TPU v7x, 32 devices: a whole 2x2x4 slice. The times are simulated.
32 devices in a mesh: fsdp: 2 (over y), ctx: 4 (over z), tp: 4 (over x, core).
Axes of the slice: x: 2, y: 2, z: 4, core: 2. Of those that a mesh axis runs over, the one named last changes fastest.
Arguments:
- latent_in: bfloat16 [4, 1024, 768], P('fsdp', 'ctx'), may hold values from -6 to 6
- condition: bfloat16 [4, 768], P('fsdp'), may hold values from -6 to 6
- ada_weight: bfloat16 [768, 6, 768], P('fsdp', None, 'tp'), may hold values from -0.21875 to 0.21875
- ada_bias: float32 [6, 768], P(None, 'tp'), may hold values from -3 to 3
- qkv_weight: bfloat16 [768, 3, 768], P('fsdp', None, 'tp'), may hold values from -0.21875 to 0.21875
- qv_bias: float32 [2, 768], P(None, 'tp'), may hold values from -3 to 3
- out_weight: bfloat16 [768, 768], P('fsdp', 'tp'), may hold values from -2.5 to 2.5
- out_bias: float32 [768], replicated, may hold values from -3 to 3
- fc1_weight: bfloat16 [768, 3072], P('fsdp', 'tp'), may hold values from -0.21875 to 0.21875
- fc1_bias: float32 [3072], P('tp'), may hold values from -3 to 3
- fc2_weight: bfloat16 [768, 3072], P('fsdp', 'tp'), may hold values from -0.109375 to 0.109375
- fc2_bias: float32 [768], replicated, may hold values from -3 to 3
- out_grad: float32 [4, 1024, 768], P('fsdp', 'ctx'), may hold values from -6 to 6
Outputs:
- block_out: float32 [4, 1024, 768], P('fsdp', 'ctx')
- latent_grad: float32 [4, 1024, 768], P('fsdp', 'ctx')
- condition_grad: float32 [4, 768], P('fsdp')
- ada_weight_grad: float32 [768, 6, 768], P('fsdp', None, 'tp')
- ada_bias_grad: float32 [6, 768], P(None, 'tp')
- qkv_weight_grad: float32 [768, 3, 768], P('fsdp', None, 'tp')
- qv_bias_grad: float32 [2, 768], P(None, 'tp')
- out_weight_grad: float32 [768, 768], P('fsdp', 'tp')
- out_bias_grad: float32 [768], replicated
- fc1_weight_grad: float32 [768, 3072], P('fsdp', 'tp')
- fc1_bias_grad: float32 [3072], P('tp')
- fc2_weight_grad: float32 [768, 3072], P('fsdp', 'tp')
- fc2_bias_grad: float32 [768], replicated
All inputs are finite; a program needn't handle non-finite values.
Results may differ from a plain program's by a relative error of at most 0.009.
The roundings to bfloat16 on the way count: a program that leaves them out, or rounds other values in their place, can miss the bound.
Values may be sent and summed in bfloat16 or wider, within the bound.
A program may use at most 128 MiB of HBM per device.

v0:
```python
import jax
import jax.numpy as jnp
from jax import lax
from jax.sharding import PartitionSpec as P

HEAD_DIM = 64
EPS = 1e-06


def dot32(left, right):
    return jnp.dot(left, right, preferred_element_type=jnp.float32)


def rows_inner(left, right):
    return lax.dot_general(
        left, right, (((0,), (0,)), ((), ())), preferred_element_type=jnp.float32
    )


def last_inner(left, right):
    return lax.dot_general(
        left, right, (((left.ndim - 1,), (1,)), ((), ())), preferred_element_type=jnp.float32
    )


def norm_rows(values):
    centre = jnp.mean(values, axis=-1, keepdims=True)
    shifted = values - centre
    spread = jnp.mean(shifted * shifted, axis=-1, keepdims=True)
    inverse = lax.rsqrt(spread + EPS)
    return (shifted * inverse, inverse)


def norm_back(grad_norm, normed, inverse):
    first = jnp.mean(grad_norm, axis=-1, keepdims=True)
    second = jnp.mean(grad_norm * normed, axis=-1, keepdims=True)
    return inverse * (grad_norm - first - normed * second)


def gelu_fn(values):
    return jax.nn.gelu(values, approximate=True)


def local(
    latent_in,
    condition,
    ada_weight,
    ada_bias,
    qkv_weight,
    qv_bias,
    out_weight,
    out_bias,
    fc1_weight,
    fc1_bias,
    fc2_weight,
    fc2_bias,
    out_grad,
):
    full_ada, full_qkv, full_out, full_fc1, full_fc2 = (
        lax.all_gather(ada_weight, "fsdp", axis=0, tiled=True),
        lax.all_gather(qkv_weight, "fsdp", axis=0, tiled=True),
        lax.all_gather(out_weight, "fsdp", axis=0, tiled=True),
        lax.all_gather(fc1_weight, "fsdp", axis=0, tiled=True),
        lax.all_gather(fc2_weight, "fsdp", axis=0, tiled=True),
    )
    lat_count, seq_part, width_all = latent_in.shape
    head_cols = full_qkv.shape[2]
    heads_here = head_cols // HEAD_DIM
    row_count = lat_count * seq_part
    att_scale = HEAD_DIM ** (-0.5)
    cond_f = condition.astype(jnp.float32)
    cond_act = jax.nn.silu(cond_f).astype(jnp.bfloat16)
    mod_cols = (
        dot32(cond_act, full_ada.reshape(width_all, 6 * head_cols)).reshape(lat_count, 6, head_cols)
        + ada_bias
    )
    modulation = lax.all_gather(mod_cols, "tp", axis=2, tiled=True)
    shift_one = modulation[:, 0][:, None, :]
    scale_one = modulation[:, 1][:, None, :]
    gate_one = modulation[:, 2][:, None, :]
    shift_two = modulation[:, 3][:, None, :]
    scale_two = modulation[:, 4][:, None, :]
    gate_two = modulation[:, 5][:, None, :]
    latent_f = latent_in.astype(jnp.float32)
    norm_one, inv_one = norm_rows(latent_f)
    input_one = (norm_one * (1.0 + scale_one) + shift_one).astype(jnp.bfloat16)
    qkv_all = dot32(
        input_one.reshape(row_count, width_all), full_qkv.reshape(width_all, 3 * head_cols)
    ).reshape(lat_count, seq_part, 3, head_cols)
    queries = (qkv_all[:, :, 0] + qv_bias[0]).astype(jnp.bfloat16)
    keys_local = qkv_all[:, :, 1].astype(jnp.bfloat16)
    values_local = (qkv_all[:, :, 2] + qv_bias[1]).astype(jnp.bfloat16)
    keys_whole, values_whole = (
        lax.all_gather(keys_local, "ctx", axis=1, tiled=True),
        lax.all_gather(values_local, "ctx", axis=1, tiled=True),
    )
    seq_whole = keys_whole.shape[1]
    q_heads = queries.reshape(lat_count, seq_part, heads_here, HEAD_DIM)
    k_heads = keys_whole.reshape(lat_count, seq_whole, heads_here, HEAD_DIM)
    v_heads = values_whole.reshape(lat_count, seq_whole, heads_here, HEAD_DIM)
    scores = (
        jnp.einsum("bqhd,bkhd->bhqk", q_heads, k_heads, preferred_element_type=jnp.float32)
        * att_scale
    )
    row_max = jnp.max(scores, axis=-1, keepdims=True)
    log_total = row_max + jnp.log(jnp.sum(jnp.exp(scores - row_max), axis=-1, keepdims=True))
    probs_half = jnp.exp(scores - log_total).astype(jnp.bfloat16)
    mixed = jnp.einsum("bhqk,bkhd->bqhd", probs_half, v_heads, preferred_element_type=jnp.float32)
    mixed = mixed.reshape(lat_count, seq_part, head_cols).astype(jnp.bfloat16)
    attn_term = last_inner(mixed, full_out)
    attn_val = lax.psum(attn_term, "tp") + out_bias
    after_attn = latent_f + gate_one * attn_val
    norm_two, inv_two = norm_rows(after_attn)
    input_two = (norm_two * (1.0 + scale_two) + shift_two).astype(jnp.bfloat16)
    hidden_pre = dot32(input_two.reshape(row_count, width_all), full_fc1) + fc1_bias
    hidden_act = gelu_fn(hidden_pre).astype(jnp.bfloat16)
    mlp_term = last_inner(hidden_act, full_fc2).reshape(lat_count, seq_part, width_all)
    mlp_val = lax.psum(mlp_term.astype(jnp.bfloat16), "tp").astype(jnp.float32) + fc2_bias
    block_out = after_attn + gate_two * mlp_val
    grad_gate_two = jnp.sum(out_grad * mlp_val, axis=1)
    grad_mlp = out_grad * gate_two
    bias_fc2 = jnp.sum(grad_mlp, axis=(0, 1))
    grad_mlp_half = grad_mlp.astype(jnp.bfloat16).reshape(row_count, width_all)
    fc2_term = rows_inner(grad_mlp_half, hidden_act)
    grad_act = dot32(grad_mlp_half, full_fc2)
    grad_pre = jax.vjp(gelu_fn, hidden_pre)[1](grad_act)[0]
    bias_fc1 = jnp.sum(grad_pre, axis=0)
    grad_pre_half = grad_pre.astype(jnp.bfloat16)
    fc1_term = rows_inner(input_two.reshape(row_count, width_all), grad_pre_half)
    input_two_term = last_inner(grad_pre_half, full_fc1).reshape(lat_count, seq_part, width_all)
    grad_input_two = lax.psum(input_two_term, "tp")
    grad_shift_two = jnp.sum(grad_input_two, axis=1)
    grad_scale_two = jnp.sum(grad_input_two * norm_two, axis=1)
    grad_after = out_grad + norm_back(grad_input_two * (1.0 + scale_two), norm_two, inv_two)
    grad_gate_one = jnp.sum(grad_after * attn_val, axis=1)
    grad_attn = grad_after * gate_one
    bias_out = jnp.sum(grad_attn, axis=(0, 1))
    grad_attn_half = grad_attn.astype(jnp.bfloat16).reshape(row_count, width_all)
    out_term = rows_inner(grad_attn_half, mixed.reshape(row_count, head_cols))
    grad_mixed = (
        dot32(grad_attn_half, full_out)
        .astype(jnp.bfloat16)
        .reshape(lat_count, seq_part, heads_here, HEAD_DIM)
    )
    scores = (
        jnp.einsum("bqhd,bkhd->bhqk", q_heads, k_heads, preferred_element_type=jnp.float32)
        * att_scale
    )
    soft_probs = jnp.exp(scores - log_total)
    probs_half = soft_probs.astype(jnp.bfloat16)
    grad_v_whole = jnp.einsum(
        "bhqk,bqhd->bkhd", probs_half, grad_mixed, preferred_element_type=jnp.float32
    )
    grad_probs = jnp.einsum(
        "bqhd,bkhd->bhqk", grad_mixed, v_heads, preferred_element_type=jnp.float32
    )
    delta = jnp.sum(soft_probs * grad_probs, axis=-1, keepdims=True)
    grad_scores = (soft_probs * (grad_probs - delta) * att_scale).astype(jnp.bfloat16)
    grad_queries = jnp.einsum(
        "bhqk,bkhd->bqhd", grad_scores, k_heads, preferred_element_type=jnp.float32
    ).reshape(lat_count, seq_part, head_cols)
    grad_k_whole = jnp.einsum(
        "bhqk,bqhd->bkhd", grad_scores, q_heads, preferred_element_type=jnp.float32
    )
    grad_keys, grad_values = (
        lax.psum_scatter(
            grad_k_whole.reshape(lat_count, seq_whole, head_cols),
            "ctx",
            scatter_dimension=1,
            tiled=True,
        ),
        lax.psum_scatter(
            grad_v_whole.reshape(lat_count, seq_whole, head_cols),
            "ctx",
            scatter_dimension=1,
            tiled=True,
        ),
    )
    bias_qv = jnp.stack([jnp.sum(grad_queries, axis=(0, 1)), jnp.sum(grad_values, axis=(0, 1))])
    grad_qkv = (
        jnp.stack([grad_queries, grad_keys, grad_values], axis=2)
        .astype(jnp.bfloat16)
        .reshape(row_count, 3 * head_cols)
    )
    qkv_term = rows_inner(input_one.reshape(row_count, width_all), grad_qkv).reshape(
        width_all, 3, head_cols
    )
    input_one_term = last_inner(grad_qkv, full_qkv.reshape(width_all, 3 * head_cols)).reshape(
        lat_count, seq_part, width_all
    )
    grad_input_one = lax.psum(input_one_term, "tp")
    grad_shift_one = jnp.sum(grad_input_one, axis=1)
    grad_scale_one = jnp.sum(grad_input_one * norm_one, axis=1)
    latent_grad = grad_after + norm_back(grad_input_one * (1.0 + scale_one), norm_one, inv_one)
    grad_mod = jnp.stack(
        [
            grad_shift_one,
            grad_scale_one,
            grad_gate_one,
            grad_shift_two,
            grad_scale_two,
            grad_gate_two,
        ],
        axis=1,
    )
    mod_part = lax.dynamic_slice_in_dim(grad_mod, lax.axis_index("tp") * head_cols, head_cols, 2)
    bias_ada = jnp.sum(mod_part, axis=0)
    cond_term = jnp.einsum(
        "bje,dje->bd", mod_part, full_ada.astype(jnp.float32), precision=lax.Precision.HIGHEST
    )
    grad_cond_act = lax.psum(cond_term, ("ctx", "tp"))
    condition_grad = jax.vjp(jax.nn.silu, cond_f)[1](grad_cond_act)[0]
    bias_grads = lax.psum((bias_ada, bias_qv, bias_out, bias_fc1, bias_fc2), ("fsdp", "ctx"))
    ada_term = jnp.einsum(
        "bd,bje->dje", cond_act.astype(jnp.float32), mod_part, precision=lax.Precision.HIGHEST
    )
    weight_terms = (ada_term, qkv_term, out_term, fc1_term, fc2_term)
    pieces = (
        lax.psum_scatter(weight_terms[0], ("fsdp", "ctx"), scatter_dimension=0, tiled=True),
        lax.psum_scatter(weight_terms[1], ("fsdp", "ctx"), scatter_dimension=0, tiled=True),
        lax.psum_scatter(weight_terms[2], ("fsdp", "ctx"), scatter_dimension=0, tiled=True),
        lax.psum_scatter(weight_terms[3], ("fsdp", "ctx"), scatter_dimension=0, tiled=True),
        lax.psum_scatter(weight_terms[4], ("fsdp", "ctx"), scatter_dimension=0, tiled=True),
    )
    weight_grads = (
        lax.all_gather(pieces[0], "ctx", axis=0, tiled=True),
        lax.all_gather(pieces[1], "ctx", axis=0, tiled=True),
        lax.all_gather(pieces[2], "ctx", axis=0, tiled=True),
        lax.all_gather(pieces[3], "ctx", axis=0, tiled=True),
        lax.all_gather(pieces[4], "ctx", axis=0, tiled=True),
    )
    return (
        block_out,
        latent_grad,
        condition_grad,
        weight_grads[0],
        bias_grads[0],
        weight_grads[1],
        bias_grads[1],
        weight_grads[2],
        bias_grads[2],
        weight_grads[3],
        bias_grads[3],
        weight_grads[4],
        bias_grads[4],
    )


def solution(mesh):
    placed = (
        P("fsdp", "ctx", None),
        P("fsdp", None),
        P("fsdp", None, "tp"),
        P(None, "tp"),
        P("fsdp", None, "tp"),
        P(None, "tp"),
        P("fsdp", "tp"),
        P(),
        P("fsdp", "tp"),
        P("tp"),
        P("fsdp", "tp"),
        P(),
        P("fsdp", "ctx", None),
    )
    return jax.shard_map(
        local,
        mesh=mesh,
        in_specs=placed,
        out_specs=(
            P("fsdp", "ctx", None),
            P("fsdp", "ctx", None),
            P("fsdp", None),
            P("fsdp", None, "tp"),
            P(None, "tp"),
            P("fsdp", None, "tp"),
            P(None, "tp"),
            P("fsdp", "tp"),
            P(),
            P("fsdp", "tp"),
            P("tp"),
            P("fsdp", "tp"),
            P(),
        ),
        check_vma=False,
    )
```

profile of v0, /device:TPU:0, one launch (start us, length us, event | category | flops | bytes accessed | tf_op | source)
XLA Modules:
  0.0 946.5 jit_solution(13427247585707043213)
XLA Ops:
  10.0 7.9 all_gather.44
  18.4 21.4 %all_gather.41 = bf16[768,3,192]{0,2,1:T(8,128)(2,1)S(1)} all-gather(bf16[384,3,192]{0,2,1:T(8,128)(2,1)S(1)} %copy-done.25), channel_id=1, replica_groups=mesh['fsdp'=2,'ctx'=4,'tp'=4] {'fsdp'}, dimensions={0}, use_global_device_ids=true | all-gather | bytes 1327104 | tf_op jit(solution)/shard_map/all_gather | solution.py:61
  39.9 9.8 %all-gather.8.cloned.1.call-done = bf16[768,6,192]{0,2,1:T(8,128)(2,1)} async-done(((bf16[384,6,192]{0,2,1:T(8,128)(2,1)}), bf16[768,6,192]{0,2,1:T(8,128)(2,1)}) %all-gather.8.cloned.1.call-update) | async-done | bytes 1769488 | tf_op jit(solution)/shard_map/all_gather | solution.py:60
  49.7 2.0 fusion.41
  51.9 8.5 all_gather.40
  60.4 5.3 fusion.91
  65.7 1.9 copy.96
  71.1 19.8 %all-gather = bf16[2,1024,1,192]{1,3,2,0:T(8,128)(2,1)S(1)} all-gather(bf16[2,256,1,192]{1,3,2,0:T(8,128)(2,1)S(1)} %slice.61), channel_id=2, replica_groups=mesh['fsdp'=2,'ctx'=4,'tp'=4] {'ctx'}, dimensions={1}, use_global_device_ids=true | all-gather | bytes 983040 | tf_op jit(solution)/shard_map/all_gather | solution.py:94
  91.0 18.0 %all_gather.42 = bf16[2,1024,192]{1,2,0:T(8,128)(2,1)S(1)} all-gather(bf16[2,256,192]{1,2,0:T(8,128)(2,1)S(1)} %fusion.52), channel_id=1, replica_groups=mesh['fsdp'=2,'ctx'=4,'tp'=4] {'ctx'}, dimensions={1}, use_global_device_ids=true | all-gather | bytes 983040 | tf_op jit(solution)/shard_map/all_gather | solution.py:95
  117.1 1.9 copy.81
  120.3 37.4 %all-reduce.6.cloned.1.call-done = f32[2,256,768]{2,1,0:T(8,128)} async-done(((f32[2,256,768]{2,1,0:T(8,128)}), f32[2,256,768]{2,1,0:T(8,128)}) %all-reduce.6.cloned.1.call-update) | async-done | bytes 1572880 | tf_op jit(solution)/shard_map/psum | solution.py:111
  157.7 1.7 fusion.90
  161.3 20.8 %all-gather.10.cloned.1.call-done = bf16[768,768]{1,0:T(8,128)(2,1)} async-done(((bf16[384,768]{1,0:T(8,128)(2,1)}), bf16[768,768]{1,0:T(8,128)(2,1)}) %all-gather.10.cloned.1.call-update) | async-done | bytes 1179664 | tf_op jit(solution)/shard_map/all_gather | solution.py:63
  182.1 3.4 convolution_add_fusion
  185.5 20.7 %all-gather.12.cloned.1.call-done = bf16[768,768]{1,0:T(8,128)(2,1)} async-done(((bf16[384,768]{1,0:T(8,128)(2,1)}), bf16[768,768]{1,0:T(8,128)(2,1)}) %all-gather.12.cloned.1.call-update) | async-done | bytes 1179664 | tf_op jit(solution)/shard_map/all_gather | solution.py:64
  206.3 3.7 convolution_convert_fusion
  211.5 33.6 %all-reduce.8.cloned.1.call-done = bf16[2,256,768]{2,1,0:T(8,128)(2,1)} async-done(((bf16[2,256,768]{2,1,0:T(8,128)(2,1)}), bf16[2,256,768]{2,1,0:T(8,128)(2,1)}) %all-reduce.8.cloned.1.call-update) | async-done | bytes 786448 | tf_op jit(solution)/shard_map/psum | solution.py:118
  245.2 2.7 multiply_reduce_fusion.8
  247.9 2.2 fusion.88
  250.1 2.0 fusion.55
  252.1 43.0 %all-reduce.10.cloned.1.call-done = f32[2,256,768]{2,1,0:T(8,128)} async-done(((f32[2,256,768]{2,1,0:T(8,128)}), f32[2,256,768]{2,1,0:T(8,128)}) %all-reduce.10.cloned.1.call-update) | async-done | bytes 1572880 | tf_op jit(solution)/shard_map/psum | solution.py:131
  295.1 2.9 multiply_reduce_fusion.3
  298.0 4.5 multiply_reduce_fusion.7
  304.3 5.2 fusion.48
  310.6 3.7 fusion.60
  314.2 18.8 %fusion.6 = f32[2,3,64,1024]{3,2,1,0:T(8,128)} fusion(f32[2,3,256,1024]{3,2,1,0:T(8,128)} %fusion.60, f32[2,3,256,1024]{3,2,1,0:T(8,128)} %copy-done, f32[2,3,256]{2,1,0:T(4,128)S(1)} %copy-done.29, f32[2,256,3,64]{1,3,2,0:T(8,128)} %bitcast.144, f32[3,64]{1,0:T(4,128)S(1)} %copy-done.42), kind=kOutput, calls=%fused_computation.8 | convolution fusion | flops 215681536 | bytes 14555904 | tf_op jit(solution)/shard_map/bhqk,bqhd->bkhd/dot_general | solution.py:162
  334.2 16.0 %bitcast_reduce_fusion = (f32[3,64]{1,0:T(4,128)S(1)}, bf16[2,3,64,256]{3,2,1,0:T(8,128)(2,1)S(1)}) fusion(bf16[2,1024,3,64]{1,3,2,0:T(8,128)(2,1)S(1)} %bitcast.138, f32[2,3,256,1024]{3,2,1,0:T(8,128)} %fusion.60, f32[2,3,256,1024]{3,2,1,0:T(8,128)} %copy-done, f32[2,3,256]{2,1,0:T(4,128)S(1)} %copy-done.29), kind=kOutput, calls=%fused_computation.76 | convolution fusion | flops 215681344 | bytes 13572864 | tf_op jit(solution)/shard_map/bhqk,bkhd->bqhd/dot_general | solution.py:159
  350.3 31.5 %reduce-scatter.8.cloned.1.call-done = f32[2,256,192]{1,2,0:T(8,128)} async-done(((f32[2,1024,192]{1,2,0:T(8,128)}), f32[2,256,192]{1,2,0:T(8,128)}) %reduce-scatter.8.cloned.1.call-update) | async-done | bytes 393232 | tf_op jit(solution)/shard_map/reduce_scatter | solution.py:166
  383.8 2.0 convolution_bitcast_fusion
  386.9 3.4 fusion.53
  391.4 3.8 fusion.87
  395.4 32.3 %all-reduce.12.cloned.1.call-done = f32[2,256,768]{2,1,0:T(8,128)} async-done(((f32[2,256,768]{2,1,0:T(8,128)}), f32[2,256,768]{2,1,0:T(8,128)}) %all-reduce.12.cloned.1.call-update) | async-done | bytes 1572880 | tf_op jit(solution)/shard_map/psum | solution.py:191
  427.7 2.2 fusion.33
  430.0 4.2 fusion.69
  436.4 64.2 %reduce-scatter.18.cloned.1.call-done = f32[96,768]{1,0:T(8,128)} async-done(((f32[768,768]{1,0:T(8,128)}), f32[96,768]{1,0:T(8,128)}) %reduce-scatter.18.cloned.1.call-update) | async-done | bytes 294928 | tf_op jit(solution)/shard_map/reduce_scatter | solution.py:222
  500.7 72.5 %reduce-scatter.20.cloned.1.call-done = f32[96,768]{1,0:T(8,128)} async-done(((f32[768,768]{1,0:T(8,128)}), f32[96,768]{1,0:T(8,128)}) %reduce-scatter.20.cloned.1.call-update) | async-done | bytes 294928 | tf_op jit(solution)/shard_map/reduce_scatter | solution.py:223
  574.0 2.3 fusion.94
  576.3 95.2 %reduce-scatter.12.cloned.1.call-done = f32[96,6,192]{2,0,1:T(8,128)} async-done(((f32[768,6,192]{2,0,1:T(8,128)}), f32[96,6,192]{2,0,1:T(8,128)}) %reduce-scatter.12.cloned.1.call-update) | async-done | bytes 442384 | tf_op jit(solution)/shard_map/reduce_scatter | solution.py:219
  671.6 66.7 %reduce-scatter.16.cloned.1.call-done = f32[96,192]{1,0:T(8,128)} async-done(((f32[768,192]{1,0:T(8,128)}), f32[96,192]{1,0:T(8,128)}) %reduce-scatter.16.cloned.1.call-update) | async-done | bytes 73744 | tf_op jit(solution)/shard_map/reduce_scatter | solution.py:221
  738.3 16.5 %all_gather.49 = f32[384,192]{1,0:T(8,128)S(1)} all-gather(f32[96,192]{1,0:T(8,128)} %reduce-scatter.16.cloned.1.call-done), channel_id=1, replica_groups=mesh['fsdp'=2,'ctx'=4,'tp'=4] {'ctx'}, dimensions={0}, use_global_device_ids=true | all-gather | bytes 368640 | tf_op jit(solution)/shard_map/all_gather | solution.py:228
  756.0 37.8 %all-reduce = (f32[6,192]{1,0:T(8,128)}, f32[2,192]{1,0:T(2,128)}, f32[768]{0:T(1024)}, f32[768]{0:T(1024)}, f32[768]{0:T(1024)}) all-reduce(f32[6,192]{1,0:T(8,128)S(1)} %dynamic-slice_reduce_fusion, f32[2,192]{1,0:T(2,128)S(1)} %pad_maximum_fusion, ...), channel_id=1, replica_groups=mesh['fsdp'=2,'ctx'=4,'tp'=4] {'fsdp','ctx'}, use_global_device_ids=true, to_apply=%region_26.27 | all-reduce | flops 3840 | bytes 30720 | tf_op jit(solution)/shard_map/psum | solution.py:213
  793.8 2.4 convolution_bitcast_fusion.2
  796.2 30.8 %psum.74 = f32[2,768]{1,0:T(2,128)S(1)} all-reduce(f32[2,768]{1,0:T(2,128)S(1)} %convolution_bitcast_fusion.2), channel_id=1, replica_groups=mesh['fsdp'=2,'ctx'=4,'tp'=4] {'ctx','tp'}, use_global_device_ids=true, to_apply=%region_23.24 | all-reduce | flops 1536 | bytes 12288 | tf_op jit(solution)/shard_map/psum | solution.py:211
  827.6 3.1 fusion.32
  830.7 43.6 %reduce-scatter.14.cloned.1.call-done = f32[96,3,192]{2,0,1:T(8,128)} async-done(((f32[768,3,192]{2,0,1:T(8,128)}), f32[96,3,192]{2,0,1:T(8,128)}) %reduce-scatter.14.cloned.1.call-update) | async-done | bytes 221200 | tf_op jit(solution)/shard_map/reduce_scatter | solution.py:220
  874.3 33.9 %all_gather.48 = f32[384,3,192]{2,0,1:T(8,128)S(1)} all-gather(f32[96,3,192]{2,0,1:T(8,128)} %reduce-scatter.14.cloned.1.call-done), channel_id=1, replica_groups=mesh['fsdp'=2,'ctx'=4,'tp'=4] {'ctx'}, dimensions={0}, use_global_device_ids=true | all-gather | bytes 1105920 | tf_op jit(solution)/shard_map/all_gather | solution.py:227
  909.5 24.9 %all-gather.14.cloned.1.call-done = f32[384,6,192]{2,0,1:T(8,128)} async-done(((f32[96,6,192]{2,0,1:T(8,128)}), f32[384,6,192]{2,0,1:T(8,128)}) %all-gather.14.cloned.1.call-update) | async-done | bytes 1769488 | tf_op jit(solution)/shard_map/all_gather | solution.py:226
  934.3 2.9 copy.88
  (197 shorter events, 37.3 us)
Async XLA Ops:
  7.2 10.7 %copy-start.1 = (bf16[2,256,768]{2,1,0:T(8,128)(2,1)S(1)}, bf16[2,256,768]{2,1,0:T(8,128)(2,1)}, u32[]{:S(2)}) copy-start(bf16[2,256,768]{2,1,0:T(8,128)(2,1)} %param.13) | copy-start | bytes 2359300
  7.2 11.2 %copy-start.25 = (bf16[384,3,192]{0,2,1:T(8,128)(2,1)S(1)}, bf16[384,3,192]{0,2,1:T(8,128)(2,1)}, u32[]{:S(2)}) copy-start(bf16[384,3,192]{0,2,1:T(8,128)(2,1)} %param.17) | copy-start | bytes 1327108
  7.2 42.5 %all-gather.8.cloned.1.call-start = ((), (), s32[]{:S(2)}) async-start(), calls=%async_computation.7 | async-start | bytes 2654208 | tf_op jit(solution)/shard_map/all_gather | solution.py:60
  7.9 149.7 %all-reduce.6.cloned.1.call-start = ((), (), s32[]{:S(2)}) async-start(), calls=%async_computation.8 | async-start | bytes 3145728 | tf_op jit(solution)/shard_map/psum | solution.py:111
  10.0 39.7 %copy-start.34 = (bf16[2,768]{1,0:T(2,128)(2,1)S(1)}, bf16[2,768]{1,0:T(2,128)(2,1)}, u32[]{:S(2)}) copy-start(bf16[2,768]{1,0:T(2,128)(2,1)} %param.14) | copy-start | bytes 9220
  10.0 39.7 %copy-start.47 = (f32[6,192]{1,0:T(8,128)S(1)}, f32[6,192]{1,0:T(8,128)}, u32[]{:S(2)}) copy-start(f32[6,192]{1,0:T(8,128)} %param.16) | copy-start | bytes 13828
  18.1 51.1 %copy-start.30 = (f32[2,256]{1,0:T(2,128)}, f32[2,256]{1,0:T(2,128)S(1)}, u32[]{:S(2)}) copy-start(f32[2,256]{1,0:T(2,128)S(1)} %broadcast_multiply_fusion.5) | copy-start | bytes 6148
  39.9 30.4 %copy-start.9 = (bf16[768,3,192]{0,2,1:T(8,128)(2,1)}, bf16[768,3,192]{0,2,1:T(8,128)(2,1)S(1)}, u32[]{:S(2)}) copy-start(bf16[768,3,192]{0,2,1:T(8,128)(2,1)S(1)} %all_gather.41) | copy-start | bytes 2654212
  39.9 29.3 %copy-start.32 = (f32[2,256]{1,0:T(2,128)}, f32[2,256]{1,0:T(2,128)S(1)}, u32[]{:S(2)}) copy-start(f32[2,256]{1,0:T(2,128)S(1)} %add_rsqrt_fusion.1) | copy-start | bytes 6148
  70.9 38.0 %copy-start.41 = (f32[3,64]{1,0:T(4,128)S(1)}, f32[3,64]{1,0:T(4,128)}, u32[]{:S(2)}) copy-start(f32[3,64]{1,0:T(4,128)} %add.180) | copy-start | bytes 2308
  71.0 39.2 %copy-start.18 = (f32[2,256,1,192]{1,3,2,0:T(8,128)}, f32[2,256,1,192]{1,3,2,0:T(8,128)S(1)}, u32[]{:S(2)}) copy-start(f32[2,256,1,192]{1,3,2,0:T(8,128)S(1)} %slice.49) | copy-start | bytes 1179652
  91.0 19.2 %copy-start.12 = (bf16[2,1024,1,192]{1,3,2,0:T(8,128)(2,1)}, bf16[2,1024,1,192]{1,3,2,0:T(8,128)(2,1)S(1)}, u32[]{:S(2)}) copy-start(bf16[2,1024,1,192]{1,3,2,0:T(8,128)(2,1)S(1)} %all-gather) | copy-start | bytes 2359300
  115.7 3.3 copy-start.11
  115.7 66.4 %all-gather.10.cloned.1.call-start = ((), (), s32[]{:S(2)}) async-start(), calls=%async_computation.9 | async-start | bytes 1769472 | tf_op jit(solution)/shard_map/all_gather | solution.py:63
  116.5 89.8 %all-gather.12.cloned.1.call-start = ((), (), s32[]{:S(2)}) async-start(), calls=%async_computation.10 | async-start | bytes 1769472 | tf_op jit(solution)/shard_map/all_gather | solution.py:64
  117.0 128.1 %all-reduce.8.cloned.1.call-start = ((), (), s32[]{:S(2)}) async-start(), calls=%async_computation.11 | async-start | bytes 1572864 | tf_op jit(solution)/shard_map/psum | solution.py:118
  159.8 22.3 %copy-start.52 = (f32[768]{0:T(1024)S(1)}, f32[768]{0:T(1024)}, u32[]{:S(2)}) copy-start(f32[768]{0:T(1024)} %param.22) | copy-start | bytes 9220
  210.0 35.2 %copy-start.44 = (f32[768]{0:T(1024)S(1)}, f32[768]{0:T(1024)}, u32[]{:S(2)}) copy-start(f32[768]{0:T(1024)} %param.24) | copy-start | bytes 9220
  210.0 85.1 %all-reduce.10.cloned.1.call-start = ((), (), s32[]{:S(2)}) async-start(), calls=%async_computation.12 | async-start | bytes 3145728 | tf_op jit(solution)/shard_map/psum | solution.py:131
  252.1 45.9 %copy-start.43 = (f32[768]{0:T(1024)S(1)}, f32[768]{0:T(1024)}, u32[]{:S(2)}) copy-start(f32[768]{0:T(1024)} %param.20) | copy-start | bytes 9220
  252.1 98.2 %reduce-scatter.10.cloned.1.call-start = ((), (), s32[]{:S(2)}) async-start(), calls=%async_computation.14 | async-start | bytes 1966080 | tf_op jit(solution)/shard_map/reduce_scatter | solution.py:172
  309.5 4.8 copy-start.29
  309.5 4.8 copy-start.42
  309.5 72.3 %reduce-scatter.8.cloned.1.call-start = ((), (), s32[]{:S(2)}) async-start(), calls=%async_computation.13 | async-start | bytes 1966080 | tf_op jit(solution)/shard_map/reduce_scatter | solution.py:166
  333.1 94.6 %all-reduce.12.cloned.1.call-start = ((), (), s32[]{:S(2)}) async-start(), calls=%async_computation.15 | async-start | bytes 3145728 | tf_op jit(solution)/shard_map/psum | solution.py:191
  350.2 33.6 %copy-start.10 = (bf16[768,3,192]{0,2,1:T(8,128)(2,1)S(1)}, bf16[768,3,192]{0,2,1:T(8,128)(2,1)}, u32[]{:S(2)}) copy-start(bf16[768,3,192]{0,2,1:T(8,128)(2,1)} %copy-done.9) | copy-start | bytes 2654212
  385.8 114.8 %reduce-scatter.18.cloned.1.call-start = ((), (), s32[]{:S(2)}) async-start(), calls=%async_computation.20 | async-start | bytes 2654208 | tf_op jit(solution)/shard_map/reduce_scatter | solution.py:222
  390.3 182.9 %reduce-scatter.20.cloned.1.call-start = ((), (), s32[]{:S(2)}) async-start(), calls=%async_computation.22 | async-start | bytes 2654208 | tf_op jit(solution)/shard_map/reduce_scatter | solution.py:223
  395.2 32.4 %copy-start.31 = (f32[2,256]{1,0:T(2,128)S(1)}, f32[2,256]{1,0:T(2,128)}, u32[]{:S(2)}) copy-start(f32[2,256]{1,0:T(2,128)} %copy-done.30) | copy-start | bytes 6148
  395.2 32.4 %copy-start.33 = (f32[2,256]{1,0:T(2,128)S(1)}, f32[2,256]{1,0:T(2,128)}, u32[]{:S(2)}) copy-start(f32[2,256]{1,0:T(2,128)} %copy-done.32) | copy-start | bytes 6148
  395.3 34.6 %copy-start.38 = (f32[2,768]{1,0:T(2,128)S(1)}, f32[2,768]{1,0:T(2,128)}, u32[]{:S(2)}) copy-start(f32[2,768]{1,0:T(2,128)} %get-tuple-element.87) | copy-start | bytes 18436
  395.3 34.6 %copy-start.40 = (f32[2,768]{1,0:T(2,128)S(1)}, f32[2,768]{1,0:T(2,128)}, u32[]{:S(2)}) copy-start(f32[2,768]{1,0:T(2,128)} %get-tuple-element.88) | copy-start | bytes 18436
  395.3 34.6 %copy-start.39 = (f32[2,768]{1,0:T(2,128)S(1)}, f32[2,768]{1,0:T(2,128)}, u32[]{:S(2)}) copy-start(f32[2,768]{1,0:T(2,128)} %get-tuple-element.78) | copy-start | bytes 18436
  395.3 34.6 %copy-start.37 = (f32[2,768]{1,0:T(2,128)S(1)}, f32[2,768]{1,0:T(2,128)}, u32[]{:S(2)}) copy-start(f32[2,768]{1,0:T(2,128)} %get-tuple-element.85) | copy-start | bytes 18436
  395.3 34.6 %copy-start.35 = (bf16[2,768]{1,0:T(2,128)(2,1)S(1)}, bf16[2,768]{1,0:T(2,128)(2,1)}, u32[]{:S(2)}) copy-start(bf16[2,768]{1,0:T(2,128)(2,1)} %param.14) | copy-start | bytes 9220
  395.3 276.2 %reduce-scatter.12.cloned.1.call-start = ((), (), s32[]{:S(2)}) async-start(), calls=%async_computation.16 | async-start | bytes 5308416 | tf_op jit(solution)/shard_map/reduce_scatter | solution.py:219
  434.2 139.1 %copy-start.15 = (bf16[2,256,3,192]{1,3,2,0:T(8,128)(2,1)S(1)}, bf16[2,256,3,192]{1,3,2,0:T(8,128)(2,1)}, u32[]{:S(2)}) copy-start(bf16[2,256,3,192]{1,3,2,0:T(8,128)(2,1)} %copy-done.14) | copy-start | bytes 1769476
  434.2 304.1 %reduce-scatter.16.cloned.1.call-start = ((), (), s32[]{:S(2)}) async-start(), calls=%async_computation.19 | async-start | bytes 884736 | tf_op jit(solution)/shard_map/reduce_scatter | solution.py:221
  436.4 394.3 %all-gather.16.cloned.1.call-start = ((), (), s32[]{:S(2)}) async-start(), calls=%async_computation.21 | async-start | bytes 1474560 | tf_op jit(solution)/shard_map/all_gather | solution.py:229
  500.7 330.1 %all-gather.18.cloned.1.call-start = ((), (), s32[]{:S(2)}) async-start(), calls=%async_computation.23 | async-start | bytes 1474560 | tf_op jit(solution)/shard_map/all_gather | solution.py:230
  573.2 301.2 %reduce-scatter.14.cloned.1.call-start = ((), (), s32[]{:S(2)}) async-start(), calls=%async_computation.18 | async-start | bytes 2654208 | tf_op jit(solution)/shard_map/reduce_scatter | solution.py:220
  576.2 179.5 %copy-start.19 = (f32[2,256,192]{1,2,0:T(8,128)S(1)}, f32[2,256,192]{1,2,0:T(8,128)}, u32[]{:S(2)}) copy-start(f32[2,256,192]{1,2,0:T(8,128)} %reduce-scatter.10.cloned.1.call-done) | copy-start | bytes 1179652
  576.3 179.7 %copy-start.45 = (f32[768]{0:T(1024)S(1)}, f32[768]{0:T(1024)}, u32[]{:S(2)}) copy-start(f32[768]{0:T(1024)} %get-tuple-element.84) | copy-start | bytes 9220
  576.3 179.7 %copy-start.46 = (f32[768]{0:T(1024)S(1)}, f32[768]{0:T(1024)}, u32[]{:S(2)}) copy-start(f32[768]{0:T(1024)} %get-tuple-element.86) | copy-start | bytes 9220
  576.3 179.7 %copy-start.49 = (f32[768]{0:T(1024)S(1)}, f32[768]{0:T(1024)}, u32[]{:S(2)}) copy-start(f32[768]{0:T(1024)} %get-tuple-element.95) | copy-start | bytes 9220
  576.3 358.0 %all-gather.14.cloned.1.call-start = ((), (), s32[]{:S(2)}) async-start(), calls=%async_computation.17 | async-start | bytes 2949120 | tf_op jit(solution)/shard_map/all_gather | solution.py:226
  754.8 72.8 %copy-start.3 = (f32[2,256,768]{2,1,0:T(8,128)S(1)}, f32[2,256,768]{2,1,0:T(8,128)}, u32[]{:S(2)}) copy-start(f32[2,256,768]{2,1,0:T(8,128)} %copy-done.2) | copy-start | bytes 4718596
  909.5 27.8 %copy-start.20 = (f32[384,768]{1,0:T(8,128)S(1)}, f32[384,768]{1,0:T(8,128)}, u32[]{:S(2)}) copy-start(f32[384,768]{1,0:T(8,128)} %all-gather.16.cloned.1.call-done) | copy-start | bytes 3538948
  (23 other events, 38.8 us)
Sparse Core Ops, SparseCore 0:
  9.5 40.0 all-gather.7
  115.8 41.8 all-reduce.5
  159.2 22.8 all-gather.9
  183.5 22.7 all-gather.11
  210.1 35.0 all-reduce.7
  252.2 42.8 all-reduce.9
  309.6 35.5 reduce-scatter.9
  347.5 34.2 reduce-scatter.7
  385.9 41.6 all-reduce.11
  431.0 69.5 reduce-scatter.17
  504.1 68.9 reduce-scatter.19
  576.7 94.8 reduce-scatter.11
  675.4 62.8 reduce-scatter.15
  739.7 30.9 all-gather.15
  772.1 29.7 all-gather.17
  805.2 69.0 reduce-scatter.13
  875.8 58.5 all-gather.13
where the time goes:
time: 948 us; the launch traced here: 946 us
  waiting for transfers between devices  598 us (63%)
  blocking collectives  195 us (21%)
  matrix products  81.3 us (9%)
  local copies, waits for them, and re-layouts  31.6 us (3%)
  other arithmetic  25.1 us (3%)
  between operations  14.6 us (2%)
    reduce_scatter x1, waiting for transfers between devices, local(): lax.psum_scatter(weight_terms[0], ('fsdp', 'ctx'), scatter_dimension=0, t...  95.2 us
    reduce_scatter x1, waiting for transfers between devices, local(): lax.psum_scatter(weight_terms[4], ('fsdp', 'ctx'), scatter_dimension=0, t...  72.5 us
    reduce_scatter x1, waiting for transfers between devices, local(): lax.psum_scatter(weight_terms[2], ('fsdp', 'ctx'), scatter_dimension=0, t...  66.7 us
    reduce_scatter x1, waiting for transfers between devices, local(): lax.psum_scatter(weight_terms[3], ('fsdp', 'ctx'), scatter_dimension=0, t...  64.2 us
    reduce_scatter x1, waiting for transfers between devices, local(): lax.psum_scatter(weight_terms[1], ('fsdp', 'ctx'), scatter_dimension=0, t...  43.6 us
    psum x1, waiting for transfers between devices, local(): grad_input_two = lax.psum(input_two_term, 'tp')  43 us
    psum x1, blocking collectives, local(): lax.psum((bias_ada, bias_qv, bias_out, bias_fc1, bias_fc2), ('fsdp', 'ctx'))  37.8 us
    psum x1, waiting for transfers between devices, local(): attn_val = lax.psum(attn_term, 'tp') + out_bias  37.4 us
  transfers between devices with their start and end apart: 17, of which 14 were waited for; matrix products, arithmetic and copies ran while one was open for 8% of the time, Pallas kernels for 0%

commit v1 on v0

--- a/solution.py
+++ b/solution.py
@@ -5,6 +5,10 @@
 
 HEAD_DIM = 64
 EPS = 1e-06
+
+
+def _lead_zones(local_values, lane_axis):
+    return jnp.sum(lax.all_gather(local_values, lane_axis), 0)
 
 
 def dot32(left, right):
@@ -108,7 +112,7 @@
     mixed = jnp.einsum("bhqk,bkhd->bqhd", probs_half, v_heads, preferred_element_type=jnp.float32)
     mixed = mixed.reshape(lat_count, seq_part, head_cols).astype(jnp.bfloat16)
     attn_term = last_inner(mixed, full_out)
-    attn_val = lax.psum(attn_term, "tp") + out_bias
+    attn_val = _lead_zones(attn_term, "tp") + out_bias
     after_attn = latent_f + gate_one * attn_val
     norm_two, inv_two = norm_rows(after_attn)
     input_two = (norm_two * (1.0 + scale_two) + shift_two).astype(jnp.bfloat16)

time: 948 us -> 958 us (1.011)
    all_gather x0 -> x1, waiting for transfers between devices: none -> 40.4 us  [_lead_zones(): return jnp.sum(lax.all_gather(local_values, lane_axis), 0)]
    psum x1 -> x0, waiting for transfers between devices: 37.4 us -> none  [local(): attn_val = lax.psum(attn_term, 'tp') + out_bias]
  transfers between devices with their start and end apart: 17 -> 17, of which waited for: 14 -> 14; matrix products, arithmetic and copies ran while one was open for 8% -> 9% of each run, Pallas kernels for 0% -> 0%
where the time goes in v1:
time: 958 us; the launch traced here: 951 us
  waiting for transfers between devices  597 us (62%)
  blocking collectives  195 us (20%)
  matrix products  81.3 us (8%)
  local copies, waits for them, and re-layouts  32.8 us (3%)
  other arithmetic  28.9 us (3%)
  between operations  14.8 us (2%)
    reduce_scatter x1, waiting for transfers between devices, local(): lax.psum_scatter(weight_terms[0], ('fsdp', 'ctx'), scatter_dimension=0, t...  95.2 us
    reduce_scatter x1, waiting for transfers between devices, local(): lax.psum_scatter(weight_terms[4], ('fsdp', 'ctx'), scatter_dimension=0, t...  72.4 us
    reduce_scatter x1, waiting for transfers between devices, local(): lax.psum_scatter(weight_terms[2], ('fsdp', 'ctx'), scatter_dimension=0, t...  66.7 us
    reduce_scatter x1, waiting for transfers between devices, local(): lax.psum_scatter(weight_terms[3], ('fsdp', 'ctx'), scatter_dimension=0, t...  64.2 us
    reduce_scatter x1, waiting for transfers between devices, local(): lax.psum_scatter(weight_terms[1], ('fsdp', 'ctx'), scatter_dimension=0, t...  43.8 us
    psum x1, waiting for transfers between devices, local(): grad_input_two = lax.psum(input_two_term, 'tp')  43 us
    all_gather x1, waiting for transfers between devices, _lead_zones(): return jnp.sum(lax.all_gather(local_values, lane_axis), 0)  40.4 us
    psum x1, blocking collectives, local(): lax.psum((bias_ada, bias_qv, bias_out, bias_fc1, bias_fc2), ('fsdp', 'ctx'))  37.8 us
  transfers between devices with their start and end apart: 17, of which 14 were waited for; matrix products, arithmetic and copies ran while one was open for 9% of the time, Pallas kernels for 0%

profile of v1, /device:TPU:0, one launch (start us, length us, event | category | flops | bytes accessed | tf_op | source)
XLA Modules:
  0.0 950.7 jit_solution(15278481020390757086)
XLA Ops:
  10.0 7.9 all_gather.50
  18.4 21.4 %all_gather.47 = bf16[768,3,192]{0,2,1:T(8,128)(2,1)S(1)} all-gather(bf16[384,3,192]{0,2,1:T(8,128)(2,1)S(1)} %copy-done.25), channel_id=1, replica_groups=mesh['fsdp'=2,'ctx'=4,'tp'=4] {'fsdp'}, dimensions={0}, use_global_device_ids=true | all-gather | bytes 1327104 | tf_op jit(solution)/shard_map/all_gather | solution.py:65
  39.9 9.8 %all-gather.10.cloned.1.call-done = bf16[768,6,192]{0,2,1:T(8,128)(2,1)} async-done(((bf16[384,6,192]{0,2,1:T(8,128)(2,1)}), bf16[768,6,192]{0,2,1:T(8,128)(2,1)}) %all-gather.10.cloned.1.call-update) | async-done | bytes 1769488 | tf_op jit(solution)/shard_map/all_gather | solution.py:64
  49.7 2.0 fusion.41
  51.9 8.5 all_gather.46
  60.4 5.4 fusion.91
  67.0 1.9 copy.78
  70.9 19.8 %all-gather = bf16[2,1024,1,192]{1,3,2,0:T(8,128)(2,1)S(1)} all-gather(bf16[2,256,1,192]{1,3,2,0:T(8,128)(2,1)S(1)} %slice.61), channel_id=2, replica_groups=mesh['fsdp'=2,'ctx'=4,'tp'=4] {'ctx'}, dimensions={1}, use_global_device_ids=true | all-gather | bytes 983040 | tf_op jit(solution)/shard_map/all_gather | solution.py:98
  90.7 18.0 %all_gather.48 = bf16[2,1024,192]{1,2,0:T(8,128)(2,1)S(1)} all-gather(bf16[2,256,192]{1,2,0:T(8,128)(2,1)S(1)} %fusion.52), channel_id=1, replica_groups=mesh['fsdp'=2,'ctx'=4,'tp'=4] {'ctx'}, dimensions={1}, use_global_device_ids=true | all-gather | bytes 983040 | tf_op jit(solution)/shard_map/all_gather | solution.py:99
  118.0 1.9 copy.81
  121.2 40.4 %all-gather.22.cloned.1.call-done = f32[8,256,768]{2,1,0:T(8,128)} async-done(((f32[2,256,768]{2,1,0:T(8,128)}), f32[8,256,768]{2,1,0:T(8,128)}) %all-gather.22.cloned.1.call-update) | async-done | bytes 6291472 | tf_op jit(solution)/shard_map/all_gather | solution.py:11
  161.6 4.5 reduce_sum.210
  169.8 16.2 %all-gather.12.cloned.1.call-done = bf16[768,768]{1,0:T(8,128)(2,1)} async-done(((bf16[384,768]{1,0:T(8,128)(2,1)}), bf16[768,768]{1,0:T(8,128)(2,1)}) %all-gather.12.cloned.1.call-update) | async-done | bytes 1179664 | tf_op jit(solution)/shard_map/all_gather | solution.py:67
  186.0 3.4 convolution_add_fusion
  189.4 20.7 %all-gather.14.cloned.1.call-done = bf16[768,768]{1,0:T(8,128)(2,1)} async-done(((bf16[384,768]{1,0:T(8,128)(2,1)}), bf16[768,768]{1,0:T(8,128)(2,1)}) %all-gather.14.cloned.1.call-update) | async-done | bytes 1179664 | tf_op jit(solution)/shard_map/all_gather | solution.py:68
  210.1 3.7 convolution_convert_fusion
  215.2 33.8 %all-reduce.5.cloned.1.call-done = bf16[2,256,768]{2,1,0:T(8,128)(2,1)} async-done(((bf16[2,256,768]{2,1,0:T(8,128)(2,1)}), bf16[2,256,768]{2,1,0:T(8,128)(2,1)}) %all-reduce.5.cloned.1.call-update) | async-done | bytes 786448 | tf_op jit(solution)/shard_map/psum | solution.py:122
  249.0 2.7 multiply_reduce_fusion.8
  251.7 2.2 fusion.88
  253.9 2.0 fusion.55
  256.0 43.0 %all-reduce.7.cloned.1.call-done = f32[2,256,768]{2,1,0:T(8,128)} async-done(((f32[2,256,768]{2,1,0:T(8,128)}), f32[2,256,768]{2,1,0:T(8,128)}) %all-reduce.7.cloned.1.call-update) | async-done | bytes 1572880 | tf_op jit(solution)/shard_map/psum | solution.py:135
  298.9 2.9 multiply_reduce_fusion.3
  301.8 4.5 multiply_reduce_fusion.7
  308.1 5.2 fusion.48
  314.4 3.7 fusion.60
  318.1 18.8 %fusion.6 = f32[2,3,64,1024]{3,2,1,0:T(8,128)} fusion(f32[2,3,256,1024]{3,2,1,0:T(8,128)} %fusion.60, f32[2,3,256,1024]{3,2,1,0:T(8,128)} %copy-done, f32[2,3,256]{2,1,0:T(4,128)S(1)} %copy-done.29, f32[2,256,3,64]{1,3,2,0:T(8,128)} %bitcast.146, f32[3,64]{1,0:T(4,128)S(1)} %copy-done.42), kind=kOutput, calls=%fused_computation.8 | convolution fusion | flops 215681536 | bytes 14555904 | tf_op jit(solution)/shard_map/bhqk,bqhd->bkhd/dot_general | solution.py:166
  338.0 16.0 %bitcast_reduce_fusion = (f32[3,64]{1,0:T(4,128)S(1)}, bf16[2,3,64,256]{3,2,1,0:T(8,128)(2,1)S(1)}) fusion(bf16[2,1024,3,64]{1,3,2,0:T(8,128)(2,1)S(1)} %bitcast.140, f32[2,3,256,1024]{3,2,1,0:T(8,128)} %fusion.60, f32[2,3,256,1024]{3,2,1,0:T(8,128)} %copy-done, f32[2,3,256]{2,1,0:T(4,128)S(1)} %copy-done.29), kind=kOutput, calls=%fused_computation.76 | convolution fusion | flops 215681344 | bytes 13572864 | tf_op jit(solution)/shard_map/bhqk,bkhd->bqhd/dot_general | solution.py:163
  354.1 31.5 %reduce-scatter.8.cloned.1.call-done = f32[2,256,192]{1,2,0:T(8,128)} async-done(((f32[2,1024,192]{1,2,0:T(8,128)}), f32[2,256,192]{1,2,0:T(8,128)}) %reduce-scatter.8.cloned.1.call-update) | async-done | bytes 393232 | tf_op jit(solution)/shard_map/reduce_scatter | solution.py:170
  387.6 2.0 convolution_bitcast_fusion
  390.7 3.4 fusion.53
  395.3 3.8 fusion.87
  399.4 32.1 %all-reduce.9.cloned.1.call-done = f32[2,256,768]{2,1,0:T(8,128)} async-done(((f32[2,256,768]{2,1,0:T(8,128)}), f32[2,256,768]{2,1,0:T(8,128)}) %all-reduce.9.cloned.1.call-update) | async-done | bytes 1572880 | tf_op jit(solution)/shard_map/psum | solution.py:195
  431.5 2.2 fusion.33
  433.8 4.2 fusion.69
  440.3 64.2 %reduce-scatter.18.cloned.1.call-done = f32[96,768]{1,0:T(8,128)} async-done(((f32[768,768]{1,0:T(8,128)}), f32[96,768]{1,0:T(8,128)}) %reduce-scatter.18.cloned.1.call-update) | async-done | bytes 294928 | tf_op jit(solution)/shard_map/reduce_scatter | solution.py:226
  504.5 72.4 %reduce-scatter.20.cloned.1.call-done = f32[96,768]{1,0:T(8,128)} async-done(((f32[768,768]{1,0:T(8,128)}), f32[96,768]{1,0:T(8,128)}) %reduce-scatter.20.cloned.1.call-update) | async-done | bytes 294928 | tf_op jit(solution)/shard_map/reduce_scatter | solution.py:227
  577.7 2.3 fusion.94
  580.1 95.2 %reduce-scatter.12.cloned.1.call-done = f32[96,6,192]{2,0,1:T(8,128)} async-done(((f32[768,6,192]{2,0,1:T(8,128)}), f32[96,6,192]{2,0,1:T(8,128)}) %reduce-scatter.12.cloned.1.call-update) | async-done | bytes 442384 | tf_op jit(solution)/shard_map/reduce_scatter | solution.py:223
  675.4 66.7 %reduce-scatter.16.cloned.1.call-done = f32[96,192]{1,0:T(8,128)} async-done(((f32[768,192]{1,0:T(8,128)}), f32[96,192]{1,0:T(8,128)}) %reduce-scatter.16.cloned.1.call-update) | async-done | bytes 73744 | tf_op jit(solution)/shard_map/reduce_scatter | solution.py:225
  742.1 16.5 %all_gather.57 = f32[384,192]{1,0:T(8,128)S(1)} all-gather(f32[96,192]{1,0:T(8,128)} %reduce-scatter.16.cloned.1.call-done), channel_id=1, replica_groups=mesh['fsdp'=2,'ctx'=4,'tp'=4] {'ctx'}, dimensions={0}, use_global_device_ids=true | all-gather | bytes 368640 | tf_op jit(solution)/shard_map/all_gather | solution.py:232
  759.7 37.8 %all-reduce = (f32[6,192]{1,0:T(8,128)}, f32[2,192]{1,0:T(2,128)}, f32[768]{0:T(1024)}, f32[768]{0:T(1024)}, f32[768]{0:T(1024)}) all-reduce(f32[6,192]{1,0:T(8,128)S(1)} %dynamic-slice_reduce_fusion, f32[2,192]{1,0:T(2,128)S(1)} %pad_maximum_fusion, ...), channel_id=1, replica_groups=mesh['fsdp'=2,'ctx'=4,'tp'=4] {'fsdp','ctx'}, use_global_device_ids=true, to_apply=%region_26.27 | all-reduce | flops 3840 | bytes 30720 | tf_op jit(solution)/shard_map/psum | solution.py:217
  797.5 2.4 convolution_bitcast_fusion.2
  800.0 30.8 %psum.66 = f32[2,768]{1,0:T(2,128)S(1)} all-reduce(f32[2,768]{1,0:T(2,128)S(1)} %convolution_bitcast_fusion.2), channel_id=1, replica_groups=mesh['fsdp'=2,'ctx'=4,'tp'=4] {'ctx','tp'}, use_global_device_ids=true, to_apply=%region_23.24 | all-reduce | flops 1536 | bytes 12288 | tf_op jit(solution)/shard_map/psum | solution.py:215
  831.4 3.1 fusion.32
  834.5 43.8 %reduce-scatter.14.cloned.1.call-done = f32[96,3,192]{2,0,1:T(8,128)} async-done(((f32[768,3,192]{2,0,1:T(8,128)}), f32[96,3,192]{2,0,1:T(8,128)}) %reduce-scatter.14.cloned.1.call-update) | async-done | bytes 221200 | tf_op jit(solution)/shard_map/reduce_scatter | solution.py:224
  878.3 33.9 %all_gather.56 = f32[384,3,192]{2,0,1:T(8,128)S(1)} all-gather(f32[96,3,192]{2,0,1:T(8,128)} %reduce-scatter.14.cloned.1.call-done), channel_id=1, replica_groups=mesh['fsdp'=2,'ctx'=4,'tp'=4] {'ctx'}, dimensions={0}, use_global_device_ids=true | all-gather | bytes 1105920 | tf_op jit(solution)/shard_map/all_gather | solution.py:231
  913.4 24.9 %all-gather.16.cloned.1.call-done = f32[384,6,192]{2,0,1:T(8,128)} async-done(((f32[96,6,192]{2,0,1:T(8,128)}), f32[384,6,192]{2,0,1:T(8,128)}) %all-gather.16.cloned.1.call-update) | async-done | bytes 1769488 | tf_op jit(solution)/shard_map/all_gather | solution.py:230
  938.3 2.9 copy.88
  (198 shorter events, 39.8 us)
Async XLA Ops:
  7.2 10.7 %copy-start.1 = (bf16[2,256,768]{2,1,0:T(8,128)(2,1)S(1)}, bf16[2,256,768]{2,1,0:T(8,128)(2,1)}, u32[]{:S(2)}) copy-start(bf16[2,256,768]{2,1,0:T(8,128)(2,1)} %param.13) | copy-start | bytes 2359300
  7.2 11.2 %copy-start.25 = (bf16[384,3,192]{0,2,1:T(8,128)(2,1)S(1)}, bf16[384,3,192]{0,2,1:T(8,128)(2,1)}, u32[]{:S(2)}) copy-start(bf16[384,3,192]{0,2,1:T(8,128)(2,1)} %param.17) | copy-start | bytes 1327108
  7.2 42.5 %all-gather.10.cloned.1.call-start = ((), (), s32[]{:S(2)}) async-start(), calls=%async_computation.7 | async-start | bytes 2654208 | tf_op jit(solution)/shard_map/all_gather | solution.py:64
  7.9 153.7 %all-gather.22.cloned.1.call-start = ((), (), s32[]{:S(2)}) async-start(), calls=%async_computation.23 | async-start | bytes 7864320 | tf_op jit(solution)/shard_map/all_gather | solution.py:11
  10.0 39.7 %copy-start.34 = (bf16[2,768]{1,0:T(2,128)(2,1)S(1)}, bf16[2,768]{1,0:T(2,128)(2,1)}, u32[]{:S(2)}) copy-start(bf16[2,768]{1,0:T(2,128)(2,1)} %param.14) | copy-start | bytes 9220
  10.0 39.7 %copy-start.47 = (f32[6,192]{1,0:T(8,128)S(1)}, f32[6,192]{1,0:T(8,128)}, u32[]{:S(2)}) copy-start(f32[6,192]{1,0:T(8,128)} %param.16) | copy-start | bytes 13828
  18.1 50.9 %copy-start.30 = (f32[2,256]{1,0:T(2,128)}, f32[2,256]{1,0:T(2,128)S(1)}, u32[]{:S(2)}) copy-start(f32[2,256]{1,0:T(2,128)S(1)} %broadcast_multiply_fusion.5) | copy-start | bytes 6148
  39.9 30.1 %copy-start.9 = (bf16[768,3,192]{0,2,1:T(8,128)(2,1)}, bf16[768,3,192]{0,2,1:T(8,128)(2,1)S(1)}, u32[]{:S(2)}) copy-start(bf16[768,3,192]{0,2,1:T(8,128)(2,1)S(1)} %all_gather.47) | copy-start | bytes 2654212
  39.9 29.1 %copy-start.32 = (f32[2,256]{1,0:T(2,128)}, f32[2,256]{1,0:T(2,128)S(1)}, u32[]{:S(2)}) copy-start(f32[2,256]{1,0:T(2,128)S(1)} %add_rsqrt_fusion.1) | copy-start | bytes 6148
  70.7 38.0 %copy-start.41 = (f32[3,64]{1,0:T(4,128)S(1)}, f32[3,64]{1,0:T(4,128)}, u32[]{:S(2)}) copy-start(f32[3,64]{1,0:T(4,128)} %add.178) | copy-start | bytes 2308
  70.8 39.1 %copy-start.18 = (f32[2,256,1,192]{1,3,2,0:T(8,128)}, f32[2,256,1,192]{1,3,2,0:T(8,128)S(1)}, u32[]{:S(2)}) copy-start(f32[2,256,1,192]{1,3,2,0:T(8,128)S(1)} %slice.49) | copy-start | bytes 1179652
  90.7 19.2 %copy-start.12 = (bf16[2,1024,1,192]{1,3,2,0:T(8,128)(2,1)}, bf16[2,1024,1,192]{1,3,2,0:T(8,128)(2,1)S(1)}, u32[]{:S(2)}) copy-start(bf16[2,1024,1,192]{1,3,2,0:T(8,128)(2,1)S(1)} %all-gather) | copy-start | bytes 2359300
  116.1 3.7 copy-start.11
  116.1 69.8 %all-gather.12.cloned.1.call-start = ((), (), s32[]{:S(2)}) async-start(), calls=%async_computation.8 | async-start | bytes 1769472 | tf_op jit(solution)/shard_map/all_gather | solution.py:67
  116.9 93.3 %all-gather.14.cloned.1.call-start = ((), (), s32[]{:S(2)}) async-start(), calls=%async_computation.9 | async-start | bytes 1769472 | tf_op jit(solution)/shard_map/all_gather | solution.py:68
  117.5 131.6 %all-reduce.5.cloned.1.call-start = ((), (), s32[]{:S(2)}) async-start(), calls=%async_computation.10 | async-start | bytes 1572864 | tf_op jit(solution)/shard_map/psum | solution.py:122
  161.6 4.5 copy-start.43
  168.2 17.8 %copy-start.52 = (f32[768]{0:T(1024)S(1)}, f32[768]{0:T(1024)}, u32[]{:S(2)}) copy-start(f32[768]{0:T(1024)} %param.22) | copy-start | bytes 9220
  213.8 35.2 %copy-start.44 = (f32[768]{0:T(1024)S(1)}, f32[768]{0:T(1024)}, u32[]{:S(2)}) copy-start(f32[768]{0:T(1024)} %param.24) | copy-start | bytes 9220
  213.9 85.0 %all-reduce.7.cloned.1.call-start = ((), (), s32[]{:S(2)}) async-start(), calls=%async_computation.11 | async-start | bytes 3145728 | tf_op jit(solution)/shard_map/psum | solution.py:135
  255.9 98.2 %reduce-scatter.10.cloned.1.call-start = ((), (), s32[]{:S(2)}) async-start(), calls=%async_computation.13 | async-start | bytes 1966080 | tf_op jit(solution)/shard_map/reduce_scatter | solution.py:176
  313.3 4.8 copy-start.29
  313.3 4.8 copy-start.42
  313.3 72.3 %reduce-scatter.8.cloned.1.call-start = ((), (), s32[]{:S(2)}) async-start(), calls=%async_computation.12 | async-start | bytes 1966080 | tf_op jit(solution)/shard_map/reduce_scatter | solution.py:170
  336.9 94.6 %all-reduce.9.cloned.1.call-start = ((), (), s32[]{:S(2)}) async-start(), calls=%async_computation.14 | async-start | bytes 3145728 | tf_op jit(solution)/shard_map/psum | solution.py:195
  354.1 33.6 %copy-start.10 = (bf16[768,3,192]{0,2,1:T(8,128)(2,1)S(1)}, bf16[768,3,192]{0,2,1:T(8,128)(2,1)}, u32[]{:S(2)}) copy-start(bf16[768,3,192]{0,2,1:T(8,128)(2,1)} %copy-done.9) | copy-start | bytes 2654212
  389.6 114.8 %reduce-scatter.18.cloned.1.call-start = ((), (), s32[]{:S(2)}) async-start(), calls=%async_computation.19 | async-start | bytes 2654208 | tf_op jit(solution)/shard_map/reduce_scatter | solution.py:226
  394.1 182.8 %reduce-scatter.20.cloned.1.call-start = ((), (), s32[]{:S(2)}) async-start(), calls=%async_computation.21 | async-start | bytes 2654208 | tf_op jit(solution)/shard_map/reduce_scatter | solution.py:227
  399.1 32.4 %copy-start.31 = (f32[2,256]{1,0:T(2,128)S(1)}, f32[2,256]{1,0:T(2,128)}, u32[]{:S(2)}) copy-start(f32[2,256]{1,0:T(2,128)} %copy-done.30) | copy-start | bytes 6148
  399.1 32.4 %copy-start.33 = (f32[2,256]{1,0:T(2,128)S(1)}, f32[2,256]{1,0:T(2,128)}, u32[]{:S(2)}) copy-start(f32[2,256]{1,0:T(2,128)} %copy-done.32) | copy-start | bytes 6148
  399.1 34.6 %copy-start.38 = (f32[2,768]{1,0:T(2,128)S(1)}, f32[2,768]{1,0:T(2,128)}, u32[]{:S(2)}) copy-start(f32[2,768]{1,0:T(2,128)} %get-tuple-element.87) | copy-start | bytes 18436
  399.1 34.6 %copy-start.40 = (f32[2,768]{1,0:T(2,128)S(1)}, f32[2,768]{1,0:T(2,128)}, u32[]{:S(2)}) copy-start(f32[2,768]{1,0:T(2,128)} %get-tuple-element.88) | copy-start | bytes 18436
  399.1 34.6 %copy-start.39 = (f32[2,768]{1,0:T(2,128)S(1)}, f32[2,768]{1,0:T(2,128)}, u32[]{:S(2)}) copy-start(f32[2,768]{1,0:T(2,128)} %get-tuple-element.78) | copy-start | bytes 18436
  399.1 34.6 %copy-start.37 = (f32[2,768]{1,0:T(2,128)S(1)}, f32[2,768]{1,0:T(2,128)}, u32[]{:S(2)}) copy-start(f32[2,768]{1,0:T(2,128)} %get-tuple-element.85) | copy-start | bytes 18436
  399.1 34.6 %copy-start.35 = (bf16[2,768]{1,0:T(2,128)(2,1)S(1)}, bf16[2,768]{1,0:T(2,128)(2,1)}, u32[]{:S(2)}) copy-start(bf16[2,768]{1,0:T(2,128)(2,1)} %param.14) | copy-start | bytes 9220
  399.2 276.1 %reduce-scatter.12.cloned.1.call-start = ((), (), s32[]{:S(2)}) async-start(), calls=%async_computation.15 | async-start | bytes 5308416 | tf_op jit(solution)/shard_map/reduce_scatter | solution.py:223
  438.0 139.0 %copy-start.15 = (bf16[2,256,3,192]{1,3,2,0:T(8,128)(2,1)S(1)}, bf16[2,256,3,192]{1,3,2,0:T(8,128)(2,1)}, u32[]{:S(2)}) copy-start(bf16[2,256,3,192]{1,3,2,0:T(8,128)(2,1)} %copy-done.14) | copy-start | bytes 1769476
  438.0 304.1 %reduce-scatter.16.cloned.1.call-start = ((), (), s32[]{:S(2)}) async-start(), calls=%async_computation.18 | async-start | bytes 884736 | tf_op jit(solution)/shard_map/reduce_scatter | solution.py:225
  440.2 394.3 %all-gather.18.cloned.1.call-start = ((), (), s32[]{:S(2)}) async-start(), calls=%async_computation.20 | async-start | bytes 1474560 | tf_op jit(solution)/shard_map/all_gather | solution.py:233
  504.5 330.0 %all-gather.20.cloned.1.call-start = ((), (), s32[]{:S(2)}) async-start(), calls=%async_computation.22 | async-start | bytes 1474560 | tf_op jit(solution)/shard_map/all_gather | solution.py:234
  576.9 301.3 %reduce-scatter.14.cloned.1.call-start = ((), (), s32[]{:S(2)}) async-start(), calls=%async_computation.17 | async-start | bytes 2654208 | tf_op jit(solution)/shard_map/reduce_scatter | solution.py:224
  580.0 179.5 %copy-start.19 = (f32[2,256,192]{1,2,0:T(8,128)S(1)}, f32[2,256,192]{1,2,0:T(8,128)}, u32[]{:S(2)}) copy-start(f32[2,256,192]{1,2,0:T(8,128)} %reduce-scatter.10.cloned.1.call-done) | copy-start | bytes 1179652
  580.0 179.7 %copy-start.45 = (f32[768]{0:T(1024)S(1)}, f32[768]{0:T(1024)}, u32[]{:S(2)}) copy-start(f32[768]{0:T(1024)} %get-tuple-element.84) | copy-start | bytes 9220
  580.0 179.7 %copy-start.46 = (f32[768]{0:T(1024)S(1)}, f32[768]{0:T(1024)}, u32[]{:S(2)}) copy-start(f32[768]{0:T(1024)} %get-tuple-element.86) | copy-start | bytes 9220
  580.0 179.7 %copy-start.49 = (f32[768]{0:T(1024)S(1)}, f32[768]{0:T(1024)}, u32[]{:S(2)}) copy-start(f32[768]{0:T(1024)} %get-tuple-element.95) | copy-start | bytes 9220
  580.0 358.3 %all-gather.16.cloned.1.call-start = ((), (), s32[]{:S(2)}) async-start(), calls=%async_computation.16 | async-start | bytes 2949120 | tf_op jit(solution)/shard_map/all_gather | solution.py:230
  758.6 72.8 %copy-start.3 = (f32[2,256,768]{2,1,0:T(8,128)S(1)}, f32[2,256,768]{2,1,0:T(8,128)}, u32[]{:S(2)}) copy-start(f32[2,256,768]{2,1,0:T(8,128)} %copy-done.2) | copy-start | bytes 4718596
  913.4 27.8 %copy-start.20 = (f32[384,768]{1,0:T(8,128)S(1)}, f32[384,768]{1,0:T(8,128)}, u32[]{:S(2)}) copy-start(f32[384,768]{1,0:T(8,128)} %all-gather.18.cloned.1.call-done) | copy-start | bytes 3538948
  (23 other events, 38.0 us)
Sparse Core Ops, SparseCore 0:
  9.5 40.0 all-gather.9
  116.3 45.3 all-gather.21
  163.2 22.7 all-gather.11
  187.4 22.7 all-gather.13
  214.0 34.9 all-reduce.4
  256.0 42.8 all-reduce.6
  313.4 35.5 reduce-scatter.9
  351.3 34.2 reduce-scatter.7
  389.7 41.6 all-reduce.8
  434.8 69.6 reduce-scatter.17
  508.0 68.8 reduce-scatter.19
  580.4 94.8 reduce-scatter.11
  679.2 62.8 reduce-scatter.15
  743.5 30.9 all-gather.17
  775.9 29.7 all-gather.19
  809.0 69.1 reduce-scatter.13
  879.7 58.5 all-gather.15
